TPU v7x, 512 devices: a whole 4x4x16 slice. The times are simulated.
512 devices in a mesh: ctx: 64 (over z, x), ch: 8 (over y, core).
Axes of the slice: x: 4, y: 4, z: 16, core: 2. Of those that a mesh axis runs over, the one named last changes fastest.
Arguments:
- gate_input: bfloat16 [16384, 4096], P('ctx', 'ch'), may hold values from -6 to 6
- key_input: bfloat16 [16384, 4096], P('ctx', 'ch'), may hold values from -6 to 6
- value_input: bfloat16 [16384, 4096], P('ctx', 'ch'), may hold values from -6 to 6
- decay_rate: float32 [16, 4096], P(None, 'ch'), may hold values from 0.00012207031 to 0.26666667
- frequency: float32 [16, 4096], P(None, 'ch'), may hold values from 0 to 2.4
- residue: float32 [2, 16, 4096], P(None, None, 'ch'), may hold values from -2 to 2
- skip_gain: float32 [4096], P('ch'), may hold values from -3 to 3
- out_weight: bfloat16 [4096, 4096], P('ctx', 'ch'), may hold values from -0.09375 to 0.09375
Outputs:
- mixed: bfloat16 [16384, 4096], P('ctx', 'ch')
All inputs are finite; a program needn't handle non-finite values.
Results may differ from a plain program's by a relative error of at most 0.014.
Values may be sent and summed in bfloat16 or wider, within the bound.
A program may use at most 128 MiB of HBM per device.

v0:
```python
import jax
import jax.numpy as jnp
from jax import lax
from jax.sharding import PartitionSpec as P


def entering(value, axis, join, neutral):
    count, mine = (lax.axis_size(axis), lax.axis_index(axis))
    pieces = jax.tree.map(lambda part: lax.all_gather(part, axis), value)
    so_far = jax.tree.map(
        lambda part, zero: jnp.full_like(part, 0) + jnp.asarray(zero, part.dtype), value, neutral
    )

    def hop(position, so_far):
        longer = join(so_far, jax.tree.map(lambda part: part[position], pieces))
        return jax.tree.map(lambda new, old: jnp.where(position < mine, new, old), longer, so_far)

    return lax.fori_loop(0, count - 1, hop, so_far)


def cmul(a_re, a_im, b_re, b_im):
    return (a_re * b_re - a_im * b_im, a_re * b_im + a_im * b_re)


def filter_tables(decay_rate, frequency, residue, block_len):
    damping = 0.125 * decay_rate
    turning = 0.125 * frequency
    scaling = jnp.sqrt(2.0 * damping)
    coef_re = scaling * residue[0]
    coef_im = scaling * residue[1]
    offsets = jnp.arange(block_len).astype(jnp.float32)

    def powers(counts):
        fading = jnp.exp(-damping[None] * counts[:, None, None])
        phase = turning[None] * counts[:, None, None]
        return (fading * jnp.cos(phase), fading * jnp.sin(phase))

    back_re, back_im = powers(block_len - 1.0 - offsets)
    ahead_re, ahead_im = powers(offsets + 1.0)
    out_re, out_im = cmul(coef_re[None], coef_im[None], ahead_re, ahead_im)
    lag_re, lag_im = powers(offsets)
    filt = jnp.sum(coef_re[None] * lag_re - coef_im[None] * lag_im, axis=1)
    places = jnp.arange(block_len)
    differ = places[:, None] - places[None, :]
    picked = jnp.take(filt, jnp.maximum(differ, 0), axis=0)
    toeplitz = jnp.where((differ >= 0)[:, :, None], picked, jnp.zeros_like(picked))
    jump_re, jump_im = powers(jnp.full((1,), block_len).astype(jnp.float32))
    return (back_re, back_im, out_re, out_im, toeplitz, jump_re[0], jump_im[0])


def chain(earlier, later):
    sum_re, sum_im = cmul(earlier[0], earlier[1], later[2], later[3])
    pow_re, pow_im = cmul(earlier[2], earlier[3], later[2], later[3])
    return (sum_re + later[0], sum_im + later[1], pow_re, pow_im)


def on_device(
    gate_input, key_input, value_input, decay_rate, frequency, residue, skip_gain, out_weight
):
    highest = lax.Precision.HIGHEST
    signal = key_input.astype(jnp.float32) * value_input.astype(jnp.float32)
    tok_len, chans = signal.shape
    block_len = 16
    block_count = tok_len // block_len
    back_re, back_im, out_re, out_im, toeplitz, jump_re, jump_im = filter_tables(
        decay_rate, frequency, residue, block_len
    )
    blocks = signal.reshape(block_count, block_len, chans)
    entry_re = jnp.einsum("snc,bsc->bnc", back_re, blocks, precision=highest)
    entry_im = jnp.einsum("snc,bsc->bnc", back_im, blocks, precision=highest)

    def advance(state, entry):
        moved_re, moved_im = cmul(jump_re, jump_im, state[0], state[1])
        grown_re, grown_im = cmul(state[2], state[3], jump_re, jump_im)
        return ((moved_re + entry[0], moved_im + entry[1], grown_re, grown_im), state)

    zeros = jnp.zeros(jump_re.shape, jnp.float32)
    ones = jnp.ones(jump_re.shape, jnp.float32)
    final, starts = lax.scan(advance, (zeros, zeros, ones, zeros), (entry_re, entry_im))
    local_re, local_im, device_re, device_im = final
    prefix = entering(
        (local_re, local_im, device_re, device_im), "ctx", chain, (zeros, zeros, ones, zeros)
    )
    incoming_re, incoming_im = (prefix[0], prefix[1])
    carried_re, carried_im = cmul(starts[2], starts[3], incoming_re[None], incoming_im[None])
    begin_re = starts[0] + carried_re
    begin_im = starts[1] + carried_im
    far = jnp.einsum("tnc,bnc->btc", out_re, begin_re, precision=highest) - jnp.einsum(
        "tnc,bnc->btc", out_im, begin_im, precision=highest
    )
    near = jnp.einsum("tsc,bsc->btc", toeplitz, blocks, precision=highest)
    conv = (near + far).reshape(tok_len, chans)
    gated = (gate_input.astype(jnp.float32) * (conv + skip_gain[None, :] * signal)).astype(
        jnp.bfloat16
    )
    whole = lax.all_gather(gated, "ch", axis=1, tiled=True)
    all_rows = lax.all_gather(out_weight, "ctx", axis=0, tiled=True)
    mixed = jnp.dot(whole, all_rows, preferred_element_type=jnp.float32)
    return mixed.astype(jnp.bfloat16)


def solution(mesh):
    placed = (
        P("ctx", "ch"),
        P("ctx", "ch"),
        P("ctx", "ch"),
        P(None, "ch"),
        P(None, "ch"),
        P(None, None, "ch"),
        P("ch"),
        P("ctx", "ch"),
    )
    return jax.shard_map(
        on_device, mesh=mesh, in_specs=placed, out_specs=P("ctx", "ch"), check_vma=False
    )
```

profile of v0, /device:TPU:8, one launch (start us, length us, event | category | flops | bytes accessed | tf_op | source)
XLA Modules:
  0.0 906.5 jit_solution(10265172625318404622)
XLA Ops:
  7.7 3.7 copy.51
  11.5 6.1 multiply_add_fusion.1
  17.6 4.1 copy.54
  21.8 9.9 %convolution_bitcast_fusion.1 = f32[16,16,512]{1,0,2:T(8,128)} fusion(f32[16,16,512]{1,0,2:T(8,128)} %copy.51, f32[16,16,512]{1,0,2:T(8,128)} %copy.54), kind=kOutput, calls=%fused_computation.21 | convolution fusion | flops 25165824 | bytes 1572864 | tf_op jit(solution)/shard_map/snc,bsc->bnc/dot_general | solution.py:69
  31.7 3.5 copy.57
  35.2 3.7 copy.56
  38.9 9.9 %convolution_bitcast_fusion = f32[16,16,512]{1,0,2:T(8,128)} fusion(f32[16,16,512]{1,0,2:T(8,128)} %copy.51, f32[16,16,512]{1,0,2:T(8,128)} %copy.56), kind=kOutput, calls=%fused_computation.20 | convolution fusion | flops 25165824 | bytes 1572864 | tf_op jit(solution)/shard_map/snc,bsc->bnc/dot_general | solution.py:70
  52.5 14.0 %while.41 = (s32[]{:T(128)}, f32[16,512]{1,0:T(8,128)S(1)}, f32[16,512]{1,0:T(8,128)S(1)}, f32[16,512]{1,0:T(8,128)S(1)}, f32[16,512]{1,0:T(8,128)S(1)}, /*index...) while((s32[]{:T(128)}, f32[16,512]{1,0:T(8,128)S(1)}, ...), condition=%wide.region_2.3_spmd.clone, body=%wide.region_1.2_spmd.clone.sunk | while | flops 180227 | bytes 655533 | solution.py:79
  73.4 4.5 copy.52
  77.9 3.6 copy.60
  81.5 3.7 copy.62
  85.2 12.3 %fusion.17 = f32[512,16,16]{2,1,0:T(8,128)} fusion(f32[16,16,512]{1,0,2:T(8,128)} %copy.51, f32[16,16,512]{1,0,2:T(8,128)} %copy.52), kind=kOutput, calls=%fused_computation.66 | convolution fusion | flops 25165824 | bytes 1572864 | tf_op jit(solution)/shard_map/tsc,bsc->btc/dot_general | solution.py:91
  97.5 115.2 %all-gather.15.cloned.1.call-done = f32[1024,512]{1,0:T(8,128)} async-done(((f32[16,512]{1,0:T(8,128)}), f32[1024,512]{1,0:T(8,128)}) %all-gather.15.cloned.1.call-update) | async-done | bytes 2097168 | tf_op jit(solution)/shard_map/all_gather | solution.py:9
  212.7 139.9 %all-gather.17.cloned.1.call-done = f32[1024,512]{1,0:T(8,128)} async-done(((f32[16,512]{1,0:T(8,128)}), f32[1024,512]{1,0:T(8,128)}) %all-gather.17.cloned.1.call-update) | async-done | bytes 2097168 | tf_op jit(solution)/shard_map/all_gather | solution.py:9
  352.6 139.9 %all-gather.19.cloned.1.call-done = f32[1024,512]{1,0:T(8,128)} async-done(((f32[16,512]{1,0:T(8,128)}), f32[1024,512]{1,0:T(8,128)}) %all-gather.19.cloned.1.call-update) | async-done | bytes 2097168 | tf_op jit(solution)/shard_map/all_gather | solution.py:9
  492.5 139.8 %all-gather.21.cloned.1.call-done = f32[1024,512]{1,0:T(8,128)} async-done(((f32[16,512]{1,0:T(8,128)}), f32[1024,512]{1,0:T(8,128)}) %all-gather.21.cloned.1.call-update) | async-done | bytes 2097168 | tf_op jit(solution)/shard_map/all_gather | solution.py:9
  632.3 54.2 %while.42 = (s32[]{:T(128)}, f32[16,512]{1,0:T(8,128)S(1)}, f32[16,512]{1,0:T(8,128)S(1)}, s32[]{:T(128)}, f32[64,16,512]{2,1,0:T(8,128)}, /*index=5*/f32[64,16,...) while((s32[]{:T(128)}, f32[16,512]{1,0:T(8,128)S(1)}, ...), condition=%wide.region_4.5_spmd.clone, body=%wide.region_3.4_spmd.clone.sunk | while | flops 98308 | bytes 262277 | solution.py:18
  686.8 3.7 copy.59
  690.4 3.6 copy.61
  694.1 9.5 %fusion.18 = f32[512,16,16]{2,1,0:T(8,128)S(1)} fusion(f32[16,16,512]{1,0,2:T(8,128)} %copy.59, f32[16,16,512]{1,0,2:T(8,128)} %copy.60), kind=kOutput, calls=%fused_computation.67 | convolution fusion | flops 25165824 | bytes 1572864 | tf_op jit(solution)/shard_map/tnc,bnc->btc/dot_general | solution.py:88
  703.6 8.5 add_bitcast_fusion
  716.5 27.5 %all-gather.11.cloned.1.call-done = bf16[256,4096]{1,0:T(8,128)(2,1)} async-done(((bf16[256,512]{1,0:T(8,128)(2,1)}), bf16[256,4096]{1,0:T(8,128)(2,1)}) %all-gather.11.cloned.1.call-update) | async-done | bytes 2097168 | tf_op jit(solution)/shard_map/all_gather | solution.py:96
  744.0 150.7 %all-gather.13.cloned.1.call-done = bf16[4096,512]{1,0:T(8,128)(2,1)} async-done(((bf16[64,512]{1,0:T(8,128)(2,1)}), bf16[4096,512]{1,0:T(8,128)(2,1)}) %all-gather.13.cloned.1.call-update) | async-done | bytes 4194320 | tf_op jit(solution)/shard_map/all_gather | solution.py:97
  894.6 4.8 convolution_convert_fusion
  (175 shorter events, 82.5 us)
Async XLA Ops:
  6.5 4.8 copy-start.11
  6.5 4.8 copy-start.12
  6.5 4.8 copy-start.10
  6.5 206.1 %all-gather.15.cloned.1.call-start = ((), (), s32[]{:S(2)}) async-start(), calls=%async_computation.2 | async-start | bytes 2129920 | tf_op jit(solution)/shard_map/all_gather | solution.py:9
  66.5 0.6 copy-start.5
  66.6 0.7 copy-start.6
  66.6 1.4 copy-start.3
  66.6 2.1 copy-start.4
  67.2 285.4 %all-gather.17.cloned.1.call-start = ((), (), s32[]{:S(2)}) async-start(), calls=%async_computation.3 | async-start | bytes 2129920 | tf_op jit(solution)/shard_map/all_gather | solution.py:9
  67.9 424.6 %all-gather.19.cloned.1.call-start = ((), (), s32[]{:S(2)}) async-start(), calls=%async_computation.4 | async-start | bytes 2129920 | tf_op jit(solution)/shard_map/all_gather | solution.py:9
  68.7 563.6 %all-gather.21.cloned.1.call-start = ((), (), s32[]{:S(2)}) async-start(), calls=%async_computation.5 | async-start | bytes 2129920 | tf_op jit(solution)/shard_map/all_gather | solution.py:9
  69.2 674.7 %all-gather.11.cloned.1.call-start = ((), (), s32[]{:S(2)}) async-start(), calls=%async_computation | async-start | bytes 2359296 | tf_op jit(solution)/shard_map/all_gather | solution.py:96
  694.1 9.5 %copy-start = (f32[512,16,16]{2,1,0:T(8,128)S(1)}, f32[512,16,16]{2,1,0:T(8,128)}, u32[]{:S(2)}) copy-start(f32[512,16,16]{2,1,0:T(8,128)} %fusion.17) | copy-start | bytes 1572868
  694.1 9.5 %copy-start.1 = (f32[16,16,512]{1,0,2:T(8,128)S(1)}, f32[16,16,512]{1,0,2:T(8,128)}, u32[]{:S(2)}) copy-start(f32[16,16,512]{1,0,2:T(8,128)} %copy.62) | copy-start | bytes 1572868
  694.1 9.5 %copy-start.2 = (f32[16,16,512]{1,0,2:T(8,128)S(1)}, f32[16,16,512]{1,0,2:T(8,128)}, u32[]{:S(2)}) copy-start(f32[16,16,512]{1,0,2:T(8,128)} %copy.61) | copy-start | bytes 1572868
  712.1 2.9 copy-start.7
  712.1 2.9 copy-start.8
  712.1 2.9 copy-start.9
  712.1 2.9 copy-start.13
  715.9 178.7 %all-gather.13.cloned.1.call-start = ((), (), s32[]{:S(2)}) async-start(), calls=%async_computation.1 | async-start | bytes 4259840 | tf_op jit(solution)/shard_map/all_gather | solution.py:97
Sparse Core Ops, SparseCore 0:
  67.3 145.3 all-gather.14
  215.6 136.9 all-gather.16
  355.5 136.9 all-gather.18
  495.3 136.9 all-gather.20
  716.0 27.8 all-gather.10
  746.8 147.8 all-gather.12
where the time goes:
time: 918 us; the launch traced here: 906 us
  waiting for transfers between devices  715 us (78%)
  other arithmetic  76.7 us (8%)
  matrix products  54.8 us (6%)
  local copies, waits for them, and re-layouts  43.3 us (5%)
  between operations  14 us (2%)
    all_gather x4, waiting for transfers between devices, entering(): pieces = jax.tree.map(lambda part: lax.all_gather(part, axis), value)  535 us
    all_gather x1, waiting for transfers between devices, on_device(): all_rows = lax.all_gather(out_weight, 'ctx', axis=0, tiled=True)  151 us
    select_n x63, other arithmetic, hop(): jnp.where(position < mine, new, old)  52.8 us
    all_gather x1, waiting for transfers between devices, on_device(): whole = lax.all_gather(gated, 'ch', axis=1, tiled=True)  27.5 us
    add x17, other arithmetic, cmul(): return (a_re * b_re - a_im * b_im, a_re * b_im + a_im * b_re)  19.1 us
  transfers between devices with their start and end apart: 6, of which 6 were waited for; matrix products, arithmetic and copies ran while one was open for 3% of the time, Pallas kernels for 0%

commit v1 on v0

--- a/solution.py
+++ b/solution.py
@@ -93,7 +93,12 @@
     gated = (gate_input.astype(jnp.float32) * (conv + skip_gain[None, :] * signal)).astype(
         jnp.bfloat16
     )
-    whole = lax.all_gather(gated, "ch", axis=1, tiled=True)
+    ring = [gated]
+    for hop_ in range(7):
+        ring.append(lax.ppermute(ring[-1], "ch", [(dev, (dev + 1) % 8) for dev in range(8)]))
+    whole = jnp.roll(
+        jnp.concatenate(ring[::-1], axis=1), (lax.axis_index("ch") + 1) * ring[0].shape[1], axis=1
+    )
     all_rows = lax.all_gather(out_weight, "ctx", axis=0, tiled=True)
     mixed = jnp.dot(whole, all_rows, preferred_element_type=jnp.float32)
     return mixed.astype(jnp.bfloat16)

time: 918 us -> 800 us (0.87)
  waiting for transfers between devices: 715 us -> 589 us
  local copies, waits for them, and re-layouts: 43.3 us -> 54.8 us
    all_gather x1, waiting for transfers between devices: 151 us -> 9.09 us  [on_device(): all_rows = lax.all_gather(out_weight, 'ctx', axis=0, tiled=True)]
    ppermute x0 -> x7, waiting for transfers between devices: none -> 40.8 us  [on_device(): lax.ppermute(ring[-1], 'ch', [(dev, (dev + 1) % 8) for dev in range(8)])]
    all_gather x1 -> x0, waiting for transfers between devices: 27.5 us -> none  [on_device(): whole = lax.all_gather(gated, 'ch', axis=1, tiled=True)]
    unnamed x30 -> x43, local copies, waits for them, and re-layouts: 7.65 us -> 19.2 us
  transfers between devices with their start and end apart: 6 -> 12, of which waited for: 6 -> 12; matrix products, arithmetic and copies ran while one was open for 3% -> 15% of each run, Pallas kernels for 0% -> 0%
where the time goes in v1:
time: 800 us; the launch traced here: 789 us
  waiting for transfers between devices  589 us (74%)
  other arithmetic  74.8 us (9%)
  local copies, waits for them, and re-layouts  54.8 us (7%)
  matrix products  54.7 us (7%)
  between operations  13.7 us (2%)
    all_gather x4, waiting for transfers between devices, entering(): pieces = jax.tree.map(lambda part: lax.all_gather(part, axis), value)  536 us
    select_n x63, other arithmetic, hop(): jnp.where(position < mine, new, old)  52.8 us
    ppermute x7, waiting for transfers between devices, on_device(): lax.ppermute(ring[-1], 'ch', [(dev, (dev + 1) % 8) for dev in range(8)])  40.8 us
    unnamed x43, local copies, waits for them, and re-layouts  19.2 us
    add x17, other arithmetic, cmul(): return (a_re * b_re - a_im * b_im, a_re * b_im + a_im * b_re)  19.1 us
  transfers between devices with their start and end apart: 12, of which 12 were waited for; matrix products, arithmetic and copies ran while one was open for 15% of the time, Pallas kernels for 0%

profile of v1, /device:TPU:8, one launch (start us, length us, event | category | flops | bytes accessed | tf_op | source)
XLA Modules:
  0.0 788.8 jit_solution(17863021051562089)
XLA Ops:
  7.6 6.1 multiply_add_fusion.1
  13.7 4.1 copy.54
  21.6 9.9 %convolution_bitcast_fusion.1 = f32[16,16,512]{1,0,2:T(8,128)} fusion(f32[16,16,512]{1,0,2:T(8,128)} %copy.51, f32[16,16,512]{1,0,2:T(8,128)} %copy.54), kind=kOutput, calls=%fused_computation.21 | convolution fusion | flops 25165824 | bytes 1572864 | tf_op jit(solution)/shard_map/snc,bsc->bnc/dot_general | solution.py:69
  38.7 9.9 %convolution_bitcast_fusion = f32[16,16,512]{1,0,2:T(8,128)} fusion(f32[16,16,512]{1,0,2:T(8,128)} %copy.51, f32[16,16,512]{1,0,2:T(8,128)} %copy.56), kind=kOutput, calls=%fused_computation.20 | convolution fusion | flops 25165824 | bytes 1572864 | tf_op jit(solution)/shard_map/snc,bsc->bnc/dot_general | solution.py:70
  52.5 14.0 %while.41 = (s32[]{:T(128)}, f32[16,512]{1,0:T(8,128)S(1)}, f32[16,512]{1,0:T(8,128)S(1)}, f32[16,512]{1,0:T(8,128)S(1)}, f32[16,512]{1,0:T(8,128)S(1)}, /*index...) while((s32[]{:T(128)}, f32[16,512]{1,0:T(8,128)S(1)}, ...), condition=%wide.region_2.3_spmd.clone, body=%wide.region_1.2_spmd.clone.sunk | while | flops 180227 | bytes 655525 | solution.py:79
  75.5 4.5 copy.52
  80.1 12.2 %fusion.23 = f32[512,16,16]{2,1,0:T(8,128)} fusion(f32[16,16,512]{1,0,2:T(8,128)} %copy.51, f32[16,16,512]{1,0,2:T(8,128)} %copy.52), kind=kOutput, calls=%fused_computation.85 | convolution fusion | flops 25165824 | bytes 1572864 | tf_op jit(solution)/shard_map/tsc,bsc->btc/dot_general | solution.py:91
  95.9 116.7 %all-gather.12.cloned.1.call-done = f32[1024,512]{1,0:T(8,128)} async-done(((f32[16,512]{1,0:T(8,128)}), f32[1024,512]{1,0:T(8,128)}) %all-gather.12.cloned.1.call-update) | async-done | bytes 2097168 | tf_op jit(solution)/shard_map/all_gather | solution.py:9
  212.6 139.9 %all-gather.14.cloned.1.call-done = f32[1024,512]{1,0:T(8,128)} async-done(((f32[16,512]{1,0:T(8,128)}), f32[1024,512]{1,0:T(8,128)}) %all-gather.14.cloned.1.call-update) | async-done | bytes 2097168 | tf_op jit(solution)/shard_map/all_gather | solution.py:9
  352.5 139.9 %all-gather.16.cloned.1.call-done = f32[1024,512]{1,0:T(8,128)} async-done(((f32[16,512]{1,0:T(8,128)}), f32[1024,512]{1,0:T(8,128)}) %all-gather.16.cloned.1.call-update) | async-done | bytes 2097168 | tf_op jit(solution)/shard_map/all_gather | solution.py:9
  492.4 139.8 %all-gather.18.cloned.1.call-done = f32[1024,512]{1,0:T(8,128)} async-done(((f32[16,512]{1,0:T(8,128)}), f32[1024,512]{1,0:T(8,128)}) %all-gather.18.cloned.1.call-update) | async-done | bytes 2097168 | tf_op jit(solution)/shard_map/all_gather | solution.py:9
  632.2 54.2 %while.42 = (s32[]{:T(128)}, f32[16,512]{1,0:T(8,128)S(1)}, f32[16,512]{1,0:T(8,128)S(1)}, s32[]{:T(128)}, f32[64,16,512]{2,1,0:T(8,128)}, /*index=5*/f32[64,16,...) while((s32[]{:T(128)}, f32[16,512]{1,0:T(8,128)S(1)}, ...), condition=%wide.region_4.5_spmd.clone, body=%wide.region_3.4_spmd.clone.sunk | while | flops 98308 | bytes 262269 | solution.py:18
  686.7 3.7 copy.59
  694.1 9.5 %fusion.24 = f32[512,16,16]{2,1,0:T(8,128)S(1)} fusion(f32[16,16,512]{1,0,2:T(8,128)} %copy.59, f32[16,16,512]{1,0,2:T(8,128)} %copy.60), kind=kOutput, calls=%fused_computation.86 | convolution fusion | flops 25165824 | bytes 1572864 | tf_op jit(solution)/shard_map/tnc,bnc->btc/dot_general | solution.py:88
  703.6 8.6 %add_bitcast_fusion = f32[16,16,512]{1,0,2:T(8,128)} fusion(f32[512,16,16]{2,1,0:T(8,128)S(1)} %copy-done, f32[512,16,16]{2,1,0:T(8,128)S(1)} %fusion.24, f32[16,16,512]{1,0,2:T(8,128)S(1)} %copy-done.2, f32[16,16,512]{1,0,2:T(8,128)S(1)} %copy-done.1), kind=kOutput, calls=%fused_computation.19 | convolution fusion | flops 25427968 | bytes 2621440 | tf_op jit(solution)/shard_map/tnc,bnc->btc/dot_general | solution.py:88
  715.2 5.8 collective-permute-done
  721.0 5.8 collective-permute-done.1
  726.8 5.8 collective-permute-done.2
  732.6 5.8 collective-permute-done.3
  738.4 5.8 collective-permute-done.4
  744.2 5.8 collective-permute-done.5
  750.0 6.0 collective-permute-done.6
  768.2 9.1 %all-gather.10.cloned.1.call-done = bf16[4096,512]{1,0:T(8,128)(2,1)} async-done(((bf16[64,512]{1,0:T(8,128)(2,1)}), bf16[4096,512]{1,0:T(8,128)(2,1)}) %all-gather.10.cloned.1.call-update) | async-done | bytes 4194320 | tf_op jit(solution)/shard_map/all_gather | solution.py:102
  777.3 4.8 fusion.6
  (200 shorter events, 113.8 us)
Async XLA Ops:
  6.5 11.3 %copy-start.9 = (bf16[256,512]{1,0:T(8,128)(2,1)S(1)}, bf16[256,512]{1,0:T(8,128)(2,1)}, u32[]{:S(2)}) copy-start(bf16[256,512]{1,0:T(8,128)(2,1)} %param.13) | copy-start | bytes 786436
  6.5 11.3 %copy-start.7 = (bf16[256,512]{1,0:T(8,128)(2,1)S(1)}, bf16[256,512]{1,0:T(8,128)(2,1)}, u32[]{:S(2)}) copy-start(bf16[256,512]{1,0:T(8,128)(2,1)} %param.14) | copy-start | bytes 786436
  6.5 206.1 %all-gather.12.cloned.1.call-start = ((), (), s32[]{:S(2)}) async-start(), calls=%async_computation.1 | async-start | bytes 2129920 | tf_op jit(solution)/shard_map/all_gather | solution.py:9
  66.5 0.7 copy-start.6
  66.5 1.4 copy-start.3
  66.5 2.1 copy-start.4
  67.1 285.4 %all-gather.14.cloned.1.call-start = ((), (), s32[]{:S(2)}) async-start(), calls=%async_computation.2 | async-start | bytes 2129920 | tf_op jit(solution)/shard_map/all_gather | solution.py:9
  67.9 424.6 %all-gather.16.cloned.1.call-start = ((), (), s32[]{:S(2)}) async-start(), calls=%async_computation.3 | async-start | bytes 2129920 | tf_op jit(solution)/shard_map/all_gather | solution.py:9
  68.6 563.6 %all-gather.18.cloned.1.call-start = ((), (), s32[]{:S(2)}) async-start(), calls=%async_computation.4 | async-start | bytes 2129920 | tf_op jit(solution)/shard_map/all_gather | solution.py:9
  69.2 708.1 %all-gather.10.cloned.1.call-start = ((), (), s32[]{:S(2)}) async-start(), calls=%async_computation | async-start | bytes 4259840 | tf_op jit(solution)/shard_map/all_gather | solution.py:102
  694.1 9.5 %copy-start = (f32[512,16,16]{2,1,0:T(8,128)S(1)}, f32[512,16,16]{2,1,0:T(8,128)}, u32[]{:S(2)}) copy-start(f32[512,16,16]{2,1,0:T(8,128)} %fusion.23) | copy-start | bytes 1572868
  694.1 9.5 %copy-start.1 = (f32[16,16,512]{1,0,2:T(8,128)S(1)}, f32[16,16,512]{1,0,2:T(8,128)}, u32[]{:S(2)}) copy-start(f32[16,16,512]{1,0,2:T(8,128)} %copy.62) | copy-start | bytes 1572868
  694.1 9.5 %copy-start.2 = (f32[16,16,512]{1,0,2:T(8,128)S(1)}, f32[16,16,512]{1,0,2:T(8,128)}, u32[]{:S(2)}) copy-start(f32[16,16,512]{1,0,2:T(8,128)} %copy.61) | copy-start | bytes 1572868
  712.1 2.9 copy-start.8
  712.1 2.9 copy-start.10
  712.1 2.9 copy-start.11
  712.1 2.9 copy-start.12
  715.2 5.8 collective-permute-start
  721.0 5.8 collective-permute-start.1
  726.8 5.8 collective-permute-start.2
  732.6 5.8 collective-permute-start.3
  738.4 5.8 collective-permute-start.4
  744.2 5.8 collective-permute-start.5
  750.0 6.0 collective-permute-start.6
  (1 other events, 0.6 us)
Sparse Core Ops, SparseCore 0:
  67.2 145.3 all-gather.11
  215.5 136.9 all-gather.13
  355.5 136.9 all-gather.15
  495.2 136.9 all-gather.17
  635.0 142.1 all-gather.9
